TPU v7x, 32 devices: a whole 2x2x4 slice. The times are simulated.
32 devices in a mesh: ctx: 4 (over y, x), head: 8 (over z, core).
Axes of the slice: x: 2, y: 2, z: 4, core: 2. Of those that a mesh axis runs over, the one named last changes fastest.
Arguments:
- queries: bfloat16 [4096, 8192], P('ctx', 'head'), may hold values from -12 to 12
- key_heads: bfloat16 [1024, 4096], P(None, 'ctx'), may hold values from -6 to 6
- value_heads: bfloat16 [1024, 4096], P(None, 'ctx'), may hold values from -6 to 6
- out_weight: bfloat16 [8192, 8192], P('head'), may hold values from -0.09375 to 0.09375
- block_order: int32 [8], replicated, may hold values from 0 to 7, each once
- doc_ids: int32 [4096], replicated, may hold values from 0 to 5, never falling along the last dimension, each value on 1 to 1024 neighbouring positions
Outputs:
- projected: bfloat16 [4096, 8192], P('ctx', 'head')
Inputs may be any that keep to these rules, and one draw needn't show every extreme that they name: Layout slot j (rows j * 512 to (j + 1) * 512 - 1 of queries and projected, the same columns of key_heads and value_heads) holds block block_order[j] of the sequence; each of 0 to 7 appears once. `doc_ids`: ids never fall along the sequence; every id is used; each document holds 1 to 1024 tokens and one holds exactly 1024.
All inputs are finite; a program needn't handle non-finite values.
Results may differ from a plain program's by a relative error of at most 0.014.
Values may be sent and summed in bfloat16 or wider, within the bound.
No kernel may reach another device: no remote copies, remote signals or barrier semaphores. Data moves between devices by JAX's collectives and lax.ppermute only.
A program may use at most 192 MiB of HBM per device.

v0:
```python
import jax
import jax.numpy as jnp
from jax import lax
from jax.sharding import PartitionSpec as P

KVH = 8
HD = 128
floor_score = -1e30


def locate(row_ids, block_order, doc_ids):
    block_len = doc_ids.shape[0] // block_order.shape[0]
    block_id = row_ids // block_len
    slot_table = jnp.arange(block_order.shape[0], dtype=jnp.int32)
    starts = jnp.sum(
        jnp.where(block_id[:, None] == slot_table[None, :], block_order[None, :], 0), axis=1
    )
    places = starts * block_len + row_ids % block_len
    return (places, jnp.take(doc_ids, places))


def attend_block(
    running, key_block, value_block, key_place, key_doc, query_heads, query_place, query_doc
):
    visible = (key_place[None, :] <= query_place[:, None]) & (
        key_doc[None, :] == query_doc[:, None]
    )
    row_top, row_total, row_accum = running
    scores = jnp.einsum(
        "thd,dk->thk", query_heads, key_block, preferred_element_type=jnp.float32
    ) * key_block.shape[0] ** (-0.5)
    scores = jnp.where(visible[:, None, :], scores, floor_score)
    new_top = jnp.maximum(row_top, jnp.max(scores, axis=2))
    factor = jnp.exp(row_top - new_top)
    weights = jnp.where(visible[:, None, :], jnp.exp(scores - new_top[:, :, None]), 0.0)
    row_total = row_total * factor + jnp.sum(weights, axis=2)
    mixed = jnp.einsum(
        "thk,dk->thd", weights.astype(jnp.bfloat16), value_block, preferred_element_type=jnp.float32
    )
    row_accum = row_accum * factor[:, :, None] + mixed
    return (new_top, row_total, row_accum)


def attend_span(
    running, key_piece, value_piece, query_heads, query_place, query_doc, block_order, doc_ids
):
    key_count = key_piece.shape[1]
    block_width = 1024
    rounds = key_count // block_width
    places, doc_list = locate(jnp.arange(key_count, dtype=jnp.int32), block_order, doc_ids)

    def one_round(round_index, current):
        offset = round_index * block_width
        return attend_block(
            current,
            lax.dynamic_slice_in_dim(key_piece, offset, block_width, 1),
            lax.dynamic_slice_in_dim(value_piece, offset, block_width, 1),
            lax.dynamic_slice_in_dim(places, offset, block_width, 0),
            lax.dynamic_slice_in_dim(doc_list, offset, block_width, 0),
            query_heads,
            query_place,
            query_doc,
        )

    return lax.fori_loop(0, rounds, one_round, running)


def normalize(running, row_count):
    row_top, row_total, row_accum = running
    return (row_accum / row_total[:, :, None]).astype(jnp.bfloat16).reshape(row_count, -1)


def shards(queries, key_heads, value_heads, out_weight, block_order, doc_ids):
    row_count = queries.shape[0]
    head_count = queries.shape[1] // HD
    group_size = lax.axis_size("head") // KVH
    lane_index = lax.axis_index("head")
    kv_start = lane_index // group_size * HD
    key_part = lax.dynamic_slice_in_dim(key_heads, kv_start, HD, 0)
    value_part = lax.dynamic_slice_in_dim(value_heads, kv_start, HD, 0)
    ctx_index = lax.axis_index("ctx")
    own_rows = ctx_index * row_count + jnp.arange(row_count, dtype=jnp.int32)
    query_place, query_doc = locate(own_rows, block_order, doc_ids)
    query_heads = queries.reshape(row_count, head_count, HD)
    running = attend_span(
        (
            jnp.full((row_count, head_count), floor_score, jnp.float32),
            jnp.zeros((row_count, head_count), jnp.float32),
            jnp.zeros((row_count, head_count, HD), jnp.float32),
        ),
        lax.all_gather(key_part, "ctx", axis=1, tiled=True),
        lax.all_gather(value_part, "ctx", axis=1, tiled=True),
        query_heads,
        query_place,
        query_doc,
        block_order,
        doc_ids,
    )
    context = normalize(running, row_count)
    partial_sum = jnp.dot(context, out_weight, preferred_element_type=jnp.float32)
    return lax.psum_scatter(
        partial_sum.astype(jnp.bfloat16), "head", scatter_dimension=1, tiled=True
    )


def solution(mesh):
    placed = (P("ctx", "head"), P(None, "ctx"), P(None, "ctx"), P("head", None), P(), P())
    return jax.shard_map(
        shards, mesh=mesh, in_specs=placed, out_specs=P("ctx", "head"), check_vma=False
    )
```

profile of v0, /device:TPU:0, one launch (start us, length us, event | category | flops | bytes accessed | tf_op | source)
XLA Modules:
  0.0 472.5 jit_solution(731710215248140285)
XLA Ops:
  6.5 0.0 copy-start
  6.5 0.0 copy-start.2
  6.5 0.0 all-gather.3.cloned.1.call-start
  6.5 1.6 copy-done
  8.1 0.8 copy.20
  9.0 0.0 all-gather.3.cloned.1.call-update
  9.0 0.0 all-gather.5.cloned.1.call-start
  9.0 1.7 constant_dynamic-slice_fusion.1
  10.7 0.0 all-gather.5.cloned.1.call-update
  10.8 0.0 reduce-scatter.2.cloned.1.call-start
  10.8 0.7 select_reduce_fusion.1
  11.6 0.8 select_reduce_fusion
  12.4 5.8 %gather_fusion.1 = s32[1024]{0:T(1024)S(1)} fusion(s32[4096]{0:T(1024)} %param.13, s32[1024]{0:T(1024)S(1)} %broadcast_clamp_fusion.1), kind=kCustom, calls=%fused_computation.1 | custom fusion | bytes 12288 | tf_op jit(solution)/shard_map/jit(_take)/gather | solution.py:19
  18.3 0.0 copy-done.2
  18.3 23.0 %gather_fusion = s32[4096]{0:T(1024)S(1)} fusion(s32[4096]{0:T(1024)S(1)} %copy-done.2, s32[4096]{0:T(1024)S(1)} %broadcast_clamp_fusion), kind=kCustom, calls=%fused_computation | custom fusion | bytes 49152 | tf_op jit(solution)/shard_map/jit(_take)/gather | solution.py:19
  41.3 2.9 copy.16
  44.2 2.4 copy.17
  46.6 0.0 all-gather.3.cloned.1.call-done
  46.6 20.5 %all-gather.5.cloned.1.call-done = bf16[128,4096]{1,0:T(8,128)(2,1)} async-done(((bf16[128,1024]{1,0:T(8,128)(2,1)}), bf16[128,4096]{1,0:T(8,128)(2,1)}) %all-gather.5.cloned.1.call-update) | async-done | bytes 1048592 | tf_op jit(solution)/shard_map/all_gather | solution.py:92
  67.1 196.0 %while.18 = (s32[]{:T(128)}, f32[1024,8]{0,1:T(8,128)S(1)}, f32[1024,8]{0,1:T(8,128)S(1)}, f32[1024,8,128]{2,0,1:T(8,128)}, s32[4096]{0:T(1024)S(1)}, /*index=5*...) while((s32[]{:T(128)}, f32[1024,8]{0,1:T(8,128)S(1)}, ...), condition=%wide.region_5.6_spmd.clone, body=%wide.region_2.5_spmd.clone.sunk | while | flops 4410351616 | bytes 116424928 | solution.py:65
  67.1 1.2 compare_and_fusion.2
  68.2 14.9 %fusion.51 = (f32[1024,8]{0,1:T(8,128)S(1)}, f32[1024,1024,8]{1,0,2:T(8,128)}) fusion(pred[1024,1024]{0,1:T(8,128)(4,1)S(1)} %compare_and_fusion.2, bf16[1024,8,128]{2,0,1:T(8,128)(2,1)} %get-tuple-element.394, bf16[128,4096]{0,1:T(8,128)(2,1)} %get-tuple-element.393, s32[]{:T(128)S(6)} %select_n.212), kind=kOutput, calls=%fused_computation.4.clone.1 | convolution fusion | flops 2172641280 | bytes 36995076 | tf_op jit(solution)/shard_map/while/body/eval_jaxpr/thd,dk->thk/dot_general | solution.py:29
  83.1 14.7 %fusion.52 = f32[1024,8]{0,1:T(8,128)S(1)} fusion(f32[1024,1024,8]{1,0,2:T(8,128)} %get-tuple-element.352, f32[1024,8]{0,1:T(8,128)S(1)} %select_maximum_fusion.2, pred[1024,1024]{0,1:T(8,128)(4,1)S(1)} %compare_and_fusion.2), kind=kLoop, calls=%fused_computation.6.clone.1 | loop fusion | flops 41934848 | bytes 34668544 | tf_op jit(solution)/shard_map/while/body/eval_jaxpr/reduce_sum | solution.py:36
  97.9 17.4 %fusion.54 = f32[1024,8,128]{2,0,1:T(8,128)} fusion(f32[1024,8,128]{2,0,1:T(8,128)} %get-tuple-element.373, f32[1024,8]{0,1:T(8,128)S(1)} %get-tuple-element.354, pred[]{:T(512)S(6)} %compare.25, f32[1024,1024,8]{1,0,2:T(8,128)} %get-tuple-element.352, f32[1024,8]{0,1:T(8,128)S(1)} %select_maximum_fusion.2, ...), kind=kOutput, calls=%fused_computation.10.clone.1 | convolution fusion | flops 2192572416 | bytes 43319300 | tf_op jit(solution)/shard_map/while/body/eval_jaxpr/thk,dk->thd/dot_general | solution.py:37
  115.4 1.2 compare_and_fusion.2
  116.6 14.9 %fusion.51 = (f32[1024,8]{0,1:T(8,128)S(1)}, f32[1024,1024,8]{1,0,2:T(8,128)}) fusion(pred[1024,1024]{0,1:T(8,128)(4,1)S(1)} %compare_and_fusion.2, bf16[1024,8,128]{2,0,1:T(8,128)(2,1)} %get-tuple-element.394, bf16[128,4096]{0,1:T(8,128)(2,1)} %get-tuple-element.393, s32[]{:T(128)S(6)} %select_n.212), kind=kOutput, calls=%fused_computation.4.clone.1 | convolution fusion | flops 2172641280 | bytes 36995076 | tf_op jit(solution)/shard_map/while/body/eval_jaxpr/thd,dk->thk/dot_general | solution.py:29
  131.4 14.7 %fusion.52 = f32[1024,8]{0,1:T(8,128)S(1)} fusion(f32[1024,1024,8]{1,0,2:T(8,128)} %get-tuple-element.352, f32[1024,8]{0,1:T(8,128)S(1)} %select_maximum_fusion.2, pred[1024,1024]{0,1:T(8,128)(4,1)S(1)} %compare_and_fusion.2), kind=kLoop, calls=%fused_computation.6.clone.1 | loop fusion | flops 41934848 | bytes 34668544 | tf_op jit(solution)/shard_map/while/body/eval_jaxpr/reduce_sum | solution.py:36
  146.2 18.4 %fusion.54 = f32[1024,8,128]{2,0,1:T(8,128)} fusion(f32[1024,8,128]{2,0,1:T(8,128)} %get-tuple-element.373, f32[1024,8]{0,1:T(8,128)S(1)} %get-tuple-element.354, pred[]{:T(512)S(6)} %compare.25, f32[1024,1024,8]{1,0,2:T(8,128)} %get-tuple-element.352, f32[1024,8]{0,1:T(8,128)S(1)} %select_maximum_fusion.2, ...), kind=kOutput, calls=%fused_computation.10.clone.1 | convolution fusion | flops 2192572416 | bytes 43319300 | tf_op jit(solution)/shard_map/while/body/eval_jaxpr/thk,dk->thd/dot_general | solution.py:37
  164.6 1.2 compare_and_fusion.2
  165.8 14.9 %fusion.51 = (f32[1024,8]{0,1:T(8,128)S(1)}, f32[1024,1024,8]{1,0,2:T(8,128)}) fusion(pred[1024,1024]{0,1:T(8,128)(4,1)S(1)} %compare_and_fusion.2, bf16[1024,8,128]{2,0,1:T(8,128)(2,1)} %get-tuple-element.394, bf16[128,4096]{0,1:T(8,128)(2,1)} %get-tuple-element.393, s32[]{:T(128)S(6)} %select_n.212), kind=kOutput, calls=%fused_computation.4.clone.1 | convolution fusion | flops 2172641280 | bytes 36995076 | tf_op jit(solution)/shard_map/while/body/eval_jaxpr/thd,dk->thk/dot_general | solution.py:29
  180.7 14.7 %fusion.52 = f32[1024,8]{0,1:T(8,128)S(1)} fusion(f32[1024,1024,8]{1,0,2:T(8,128)} %get-tuple-element.352, f32[1024,8]{0,1:T(8,128)S(1)} %select_maximum_fusion.2, pred[1024,1024]{0,1:T(8,128)(4,1)S(1)} %compare_and_fusion.2), kind=kLoop, calls=%fused_computation.6.clone.1 | loop fusion | flops 41934848 | bytes 34668544 | tf_op jit(solution)/shard_map/while/body/eval_jaxpr/reduce_sum | solution.py:36
  195.4 18.4 %fusion.54 = f32[1024,8,128]{2,0,1:T(8,128)} fusion(f32[1024,8,128]{2,0,1:T(8,128)} %get-tuple-element.373, f32[1024,8]{0,1:T(8,128)S(1)} %get-tuple-element.354, pred[]{:T(512)S(6)} %compare.25, f32[1024,1024,8]{1,0,2:T(8,128)} %get-tuple-element.352, f32[1024,8]{0,1:T(8,128)S(1)} %select_maximum_fusion.2, ...), kind=kOutput, calls=%fused_computation.10.clone.1 | convolution fusion | flops 2192572416 | bytes 43319300 | tf_op jit(solution)/shard_map/while/body/eval_jaxpr/thk,dk->thd/dot_general | solution.py:37
  213.8 1.2 compare_and_fusion.2
  215.0 14.9 %fusion.51 = (f32[1024,8]{0,1:T(8,128)S(1)}, f32[1024,1024,8]{1,0,2:T(8,128)}) fusion(pred[1024,1024]{0,1:T(8,128)(4,1)S(1)} %compare_and_fusion.2, bf16[1024,8,128]{2,0,1:T(8,128)(2,1)} %get-tuple-element.394, bf16[128,4096]{0,1:T(8,128)(2,1)} %get-tuple-element.393, s32[]{:T(128)S(6)} %select_n.212), kind=kOutput, calls=%fused_computation.4.clone.1 | convolution fusion | flops 2172641280 | bytes 36995076 | tf_op jit(solution)/shard_map/while/body/eval_jaxpr/thd,dk->thk/dot_general | solution.py:29
  229.9 14.7 %fusion.52 = f32[1024,8]{0,1:T(8,128)S(1)} fusion(f32[1024,1024,8]{1,0,2:T(8,128)} %get-tuple-element.352, f32[1024,8]{0,1:T(8,128)S(1)} %select_maximum_fusion.2, pred[1024,1024]{0,1:T(8,128)(4,1)S(1)} %compare_and_fusion.2), kind=kLoop, calls=%fused_computation.6.clone.1 | loop fusion | flops 41934848 | bytes 34668544 | tf_op jit(solution)/shard_map/while/body/eval_jaxpr/reduce_sum | solution.py:36
  244.6 18.4 %fusion.54 = f32[1024,8,128]{2,0,1:T(8,128)} fusion(f32[1024,8,128]{2,0,1:T(8,128)} %get-tuple-element.373, f32[1024,8]{0,1:T(8,128)S(1)} %get-tuple-element.354, pred[]{:T(512)S(6)} %compare.25, f32[1024,1024,8]{1,0,2:T(8,128)} %get-tuple-element.352, f32[1024,8]{0,1:T(8,128)S(1)} %select_maximum_fusion.2, ...), kind=kOutput, calls=%fused_computation.10.clone.1 | convolution fusion | flops 2192572416 | bytes 43319300 | tf_op jit(solution)/shard_map/while/body/eval_jaxpr/thk,dk->thd/dot_general | solution.py:37
  263.0 5.5 %copy.18 = f32[1024,8,128]{0,2,1:T(8,128)} copy(f32[1024,8,128]{2,0,1:T(8,128)} %get-tuple-element.190) | data formatting | bytes 8388608 | tf_op jit(solution)/shard_map/while | solution.py:65
  268.6 2.8 divide_convert_fusion
  271.4 26.2 %convolution_convert_fusion = bf16[1024,8192]{1,0:T(8,128)(2,1)} fusion(bf16[1024,1024]{0,1:T(8,128)(2,1)S(1)} %bitcast.43, bf16[1024,8192]{1,0:T(8,128)(2,1)} %param.11), kind=kOutput, calls=%fused_computation.26 | convolution fusion | flops 17188257792 | bytes 35651584 | tf_op jit(solution)/shard_map/dot_general | solution.py:100
  297.5 0.0 copy-start.1
  297.5 0.0 reduce-scatter.2.cloned.1.call-update
  297.6 168.4 %reduce-scatter.2.cloned.1.call-done = bf16[1024,1024]{1,0:T(8,128)(2,1)} async-done(((bf16[1024,8192]{1,0:T(8,128)(2,1)}), bf16[1024,1024]{1,0:T(8,128)(2,1)}) %reduce-scatter.2.cloned.1.call-update) | async-done | bytes 2097168 | tf_op jit(solution)/shard_map/reduce_scatter | solution.py:101
  466.0 0.0 copy-done.1
  (34 shorter events, 0.3 us)
Async XLA Ops:
  6.5 1.6 copy-start
  6.5 11.7 %copy-start.2 = (s32[4096]{0:T(1024)S(1)}, s32[4096]{0:T(1024)}, u32[]{:S(2)}) copy-start(s32[4096]{0:T(1024)} %param.13) | copy-start | bytes 49156
  6.5 40.1 %all-gather.3.cloned.1.call-start = ((), (), s32[]{:S(2)}) async-start(), calls=%async_computation.1 | async-start | bytes 1310720 | tf_op jit(solution)/shard_map/all_gather | solution.py:91
  9.0 58.1 %all-gather.5.cloned.1.call-start = ((), (), s32[]{:S(2)}) async-start(), calls=%async_computation.2 | async-start | bytes 1310720 | tf_op jit(solution)/shard_map/all_gather | solution.py:92
  10.8 455.2 %reduce-scatter.2.cloned.1.call-start = ((), (), s32[]{:S(2)}) async-start(), calls=%async_computation.3 | async-start | bytes 18874368 | tf_op jit(solution)/shard_map/reduce_scatter | solution.py:101
  297.5 168.4 %copy-start.1 = (bf16[1024,1024]{1,0:T(8,128)(2,1)S(1)}, bf16[1024,1024]{1,0:T(8,128)(2,1)}, u32[]{:S(2)}) copy-start(bf16[1024,1024]{1,0:T(8,128)(2,1)} %param.9) | copy-start | bytes 6291460
Sparse Core Ops, SparseCore 0:
  9.2 29.3 all-gather.2
  40.4 26.6 all-gather.4
  297.7 168.2 reduce-scatter.1
where the time goes:
time: 474 us; the launch traced here: 472 us
  waiting for transfers between devices  189 us (40%)
  matrix products  158 us (33%)
  other arithmetic  68.1 us (14%)
  local copies, waits for them, and re-layouts  43.7 us (9%)
  between operations  13.3 us (3%)
    reduce_scatter x1, waiting for transfers between devices, shards(): lax.psum_scatter(partial_sum.astype(jnp.bfloat16), 'head', scatter_dimens...  168 us
    dot_general x4, matrix products, attend_block(): jnp.einsum('thk,dk->thd', weights.astype(jnp.bfloat16), value_block, pref...  72.6 us
    dot_general x4, matrix products, attend_block(): jnp.einsum('thd,dk->thk', query_heads, key_block, preferred_element_type=...  59.5 us
    reduce_sum x4, other arithmetic, attend_block(): row_total = row_total * factor + jnp.sum(weights, axis=2)  58.8 us
    gather x2, local copies, waits for them, and re-layouts, locate(): return (places, jnp.take(doc_ids, places))  28.8 us
    dot_general x1, matrix products, shards(): jnp.dot(context, out_weight, preferred_element_type=jnp.float32)  26.2 us
    all_gather x1, waiting for transfers between devices, shards(): lax.all_gather(value_part, 'ctx', axis=1, tiled=True)  20.5 us
  transfers between devices with their start and end apart: 3, of which 2 were waited for; matrix products, arithmetic and copies ran while one was open for 8% of the time, Pallas kernels for 0%

commit v1 on v0

--- a/solution.py
+++ b/solution.py
@@ -82,6 +82,24 @@
     own_rows = ctx_index * row_count + jnp.arange(row_count, dtype=jnp.int32)
     query_place, query_doc = locate(own_rows, block_order, doc_ids)
     query_heads = queries.reshape(row_count, head_count, HD)
+
+    def pack_cycles(panel, chip_axis):
+        t1, o_now, then = (lax.psum(1, chip_axis), lax.axis_index(chip_axis), panel.shape[1])
+        front, carry_out = (panel, 1)
+        while carry_out < t1:
+            front = jnp.concatenate(
+                [
+                    front,
+                    lax.ppermute(
+                        front, chip_axis, list(map(lambda s: (s, (s - carry_out) % t1), range(t1)))
+                    ),
+                ],
+                1,
+            )
+            carry_out = 2 * carry_out
+        d_next = jnp.roll(front, o_now * then, axis=1)
+        return d_next
+
     running = attend_span(
         (
             jnp.full((row_count, head_count), floor_score, jnp.float32),
@@ -89,7 +107,7 @@
             jnp.zeros((row_count, head_count, HD), jnp.float32),
         ),
         lax.all_gather(key_part, "ctx", axis=1, tiled=True),
-        lax.all_gather(value_part, "ctx", axis=1, tiled=True),
+        pack_cycles(value_part, "ctx"),
         query_heads,
         query_place,
         query_doc,

time: 474 us -> 465 us (0.981)
  waiting for transfers between devices: 189 us -> 169 us
  local copies, waits for them, and re-layouts: 43.7 us -> 49.5 us
    all_gather x1 -> x0, waiting for transfers between devices: 20.5 us -> none  [shards(): lax.all_gather(value_part, 'ctx', axis=1, tiled=True)]
    unnamed x9 -> x14, local copies, waits for them, and re-layouts: 7.66 us -> 12.5 us
  transfers between devices with their start and end apart: 3 -> 4, of which waited for: 2 -> 1; matrix products, arithmetic and copies ran while one was open for 8% -> 9% of each run, Pallas kernels for 0% -> 0%
where the time goes in v1:
time: 465 us; the launch traced here: 464 us
  waiting for transfers between devices  169 us (36%)
  matrix products  158 us (34%)
  other arithmetic  68.9 us (15%)
  local copies, waits for them, and re-layouts  49.5 us (11%)
  between operations  13.6 us (3%)
    reduce_scatter x1, waiting for transfers between devices, shards(): lax.psum_scatter(partial_sum.astype(jnp.bfloat16), 'head', scatter_dimens...  169 us
    dot_general x4, matrix products, attend_block(): jnp.einsum('thk,dk->thd', weights.astype(jnp.bfloat16), value_block, pref...  72.3 us
    dot_general x4, matrix products, attend_block(): jnp.einsum('thd,dk->thk', query_heads, key_block, preferred_element_type=...  59.5 us
    reduce_sum x4, other arithmetic, attend_block(): row_total = row_total * factor + jnp.sum(weights, axis=2)  58.8 us
    gather x2, local copies, waits for them, and re-layouts, locate(): return (places, jnp.take(doc_ids, places))  29.2 us
    dot_general x1, matrix products, shards(): jnp.dot(context, out_weight, preferred_element_type=jnp.float32)  26.2 us
    unnamed x14, local copies, waits for them, and re-layouts  12.5 us
  transfers between devices with their start and end apart: 4, of which 1 were waited for; matrix products, arithmetic and copies ran while one was open for 9% of the time, Pallas kernels for 0%

profile of v1, /device:TPU:0, one launch (start us, length us, event | category | flops | bytes accessed | tf_op | source)
XLA Modules:
  0.0 463.9 jit_solution(16658940914059973559)
XLA Ops:
  6.5 0.0 copy-start
  6.5 1.6 copy-done
  8.1 0.8 copy.20
  9.0 0.0 all-gather.2.cloned.1.call-update
  9.0 0.0 reduce-scatter.2.cloned.1.call-start
  9.1 1.8 constant_dynamic-update-slice_fusion.5
  10.8 3.9 collective-permute-start
  14.7 0.7 select_reduce_fusion.1
  15.5 0.8 select_reduce_fusion
  16.4 6.2 %gather_fusion.1 = s32[1024]{0:T(1024)S(1)} fusion(s32[4096]{0:T(1024)S(1)} %copy-done.2, s32[1024]{0:T(1024)S(1)} %broadcast_clamp_fusion.1), kind=kCustom, calls=%fused_computation.1 | custom fusion | bytes 12288 | tf_op jit(solution)/shard_map/jit(_take)/gather | solution.py:19
  22.5 0.0 collective-permute-done
  22.6 0.8 pad_maximum_fusion
  23.4 0.5 collective-permute-start.1
  24.0 23.0 %gather_fusion = s32[4096]{0:T(1024)S(1)} fusion(s32[4096]{0:T(1024)S(1)} %copy-done.2, s32[4096]{0:T(1024)S(1)} %broadcast_clamp_fusion), kind=kCustom, calls=%fused_computation | custom fusion | bytes 49152 | tf_op jit(solution)/shard_map/jit(_take)/gather | solution.py:19
  47.0 2.9 copy.16
  49.9 2.4 copy.17
  52.3 0.7 constant_dynamic-update-slice_fusion.4
  53.0 0.0 collective-permute-done.1
  53.0 0.9 constant_dynamic-update-slice_fusion.3
  53.9 0.7 constant_dynamic-update-slice_fusion.2
  54.6 0.8 constant_dynamic-update-slice_fusion.1
  55.3 0.9 constant_dynamic-update-slice_fusion
  56.2 1.3 constant_dynamic-slice_fusion.2
  57.6 0.0 all-gather.2.cloned.1.call-done
  57.6 195.7 %while.18 = (s32[]{:T(128)}, f32[1024,8]{0,1:T(8,128)S(1)}, f32[1024,8]{0,1:T(8,128)S(1)}, f32[1024,8,128]{2,0,1:T(8,128)}, s32[4096]{0:T(1024)S(1)}, /*index=5*...) while((s32[]{:T(128)}, f32[1024,8]{0,1:T(8,128)S(1)}, ...), condition=%wide.region_5.6_spmd.clone, body=%wide.region_2.5_spmd.clone.sunk | while | flops 4410351616 | bytes 116424928 | solution.py:65
  57.6 1.2 compare_and_fusion.2
  58.8 14.9 %fusion.51 = (f32[1024,8]{0,1:T(8,128)S(1)}, f32[1024,1024,8]{1,0,2:T(8,128)}) fusion(pred[1024,1024]{0,1:T(8,128)(4,1)S(1)} %compare_and_fusion.2, bf16[1024,8,128]{2,0,1:T(8,128)(2,1)} %get-tuple-element.396, bf16[128,4096]{0,1:T(8,128)(2,1)} %get-tuple-element.395, s32[]{:T(128)S(6)} %select_n.226), kind=kOutput, calls=%fused_computation.4.clone.1 | convolution fusion | flops 2172641280 | bytes 36995076 | tf_op jit(solution)/shard_map/while/body/eval_jaxpr/thd,dk->thk/dot_general | solution.py:29
  73.7 14.7 %fusion.52 = f32[1024,8]{0,1:T(8,128)S(1)} fusion(f32[1024,1024,8]{1,0,2:T(8,128)} %get-tuple-element.354, f32[1024,8]{0,1:T(8,128)S(1)} %select_maximum_fusion.2, pred[1024,1024]{0,1:T(8,128)(4,1)S(1)} %compare_and_fusion.2), kind=kLoop, calls=%fused_computation.6.clone.1 | loop fusion | flops 41934848 | bytes 34668544 | tf_op jit(solution)/shard_map/while/body/eval_jaxpr/reduce_sum | solution.py:36
  88.5 17.4 %fusion.54 = f32[1024,8,128]{2,0,1:T(8,128)} fusion(f32[1024,8,128]{2,0,1:T(8,128)} %get-tuple-element.375, f32[1024,8]{0,1:T(8,128)S(1)} %get-tuple-element.356, pred[]{:T(512)S(6)} %compare.26, f32[1024,1024,8]{1,0,2:T(8,128)} %get-tuple-element.354, f32[1024,8]{0,1:T(8,128)S(1)} %select_maximum_fusion.2, ...), kind=kOutput, calls=%fused_computation.10.clone.1 | convolution fusion | flops 2192572416 | bytes 43319300 | tf_op jit(solution)/shard_map/while/body/eval_jaxpr/thk,dk->thd/dot_general | solution.py:37
  105.9 1.2 compare_and_fusion.2
  107.1 14.9 %fusion.51 = (f32[1024,8]{0,1:T(8,128)S(1)}, f32[1024,1024,8]{1,0,2:T(8,128)}) fusion(pred[1024,1024]{0,1:T(8,128)(4,1)S(1)} %compare_and_fusion.2, bf16[1024,8,128]{2,0,1:T(8,128)(2,1)} %get-tuple-element.396, bf16[128,4096]{0,1:T(8,128)(2,1)} %get-tuple-element.395, s32[]{:T(128)S(6)} %select_n.226), kind=kOutput, calls=%fused_computation.4.clone.1 | convolution fusion | flops 2172641280 | bytes 36995076 | tf_op jit(solution)/shard_map/while/body/eval_jaxpr/thd,dk->thk/dot_general | solution.py:29
  122.0 14.7 %fusion.52 = f32[1024,8]{0,1:T(8,128)S(1)} fusion(f32[1024,1024,8]{1,0,2:T(8,128)} %get-tuple-element.354, f32[1024,8]{0,1:T(8,128)S(1)} %select_maximum_fusion.2, pred[1024,1024]{0,1:T(8,128)(4,1)S(1)} %compare_and_fusion.2), kind=kLoop, calls=%fused_computation.6.clone.1 | loop fusion | flops 41934848 | bytes 34668544 | tf_op jit(solution)/shard_map/while/body/eval_jaxpr/reduce_sum | solution.py:36
  136.7 18.3 %fusion.54 = f32[1024,8,128]{2,0,1:T(8,128)} fusion(f32[1024,8,128]{2,0,1:T(8,128)} %get-tuple-element.375, f32[1024,8]{0,1:T(8,128)S(1)} %get-tuple-element.356, pred[]{:T(512)S(6)} %compare.26, f32[1024,1024,8]{1,0,2:T(8,128)} %get-tuple-element.354, f32[1024,8]{0,1:T(8,128)S(1)} %select_maximum_fusion.2, ...), kind=kOutput, calls=%fused_computation.10.clone.1 | convolution fusion | flops 2192572416 | bytes 43319300 | tf_op jit(solution)/shard_map/while/body/eval_jaxpr/thk,dk->thd/dot_general | solution.py:37
  155.1 1.2 compare_and_fusion.2
  156.3 14.9 %fusion.51 = (f32[1024,8]{0,1:T(8,128)S(1)}, f32[1024,1024,8]{1,0,2:T(8,128)}) fusion(pred[1024,1024]{0,1:T(8,128)(4,1)S(1)} %compare_and_fusion.2, bf16[1024,8,128]{2,0,1:T(8,128)(2,1)} %get-tuple-element.396, bf16[128,4096]{0,1:T(8,128)(2,1)} %get-tuple-element.395, s32[]{:T(128)S(6)} %select_n.226), kind=kOutput, calls=%fused_computation.4.clone.1 | convolution fusion | flops 2172641280 | bytes 36995076 | tf_op jit(solution)/shard_map/while/body/eval_jaxpr/thd,dk->thk/dot_general | solution.py:29
  171.1 14.7 %fusion.52 = f32[1024,8]{0,1:T(8,128)S(1)} fusion(f32[1024,1024,8]{1,0,2:T(8,128)} %get-tuple-element.354, f32[1024,8]{0,1:T(8,128)S(1)} %select_maximum_fusion.2, pred[1024,1024]{0,1:T(8,128)(4,1)S(1)} %compare_and_fusion.2), kind=kLoop, calls=%fused_computation.6.clone.1 | loop fusion | flops 41934848 | bytes 34668544 | tf_op jit(solution)/shard_map/while/body/eval_jaxpr/reduce_sum | solution.py:36
  185.9 18.3 %fusion.54 = f32[1024,8,128]{2,0,1:T(8,128)} fusion(f32[1024,8,128]{2,0,1:T(8,128)} %get-tuple-element.375, f32[1024,8]{0,1:T(8,128)S(1)} %get-tuple-element.356, pred[]{:T(512)S(6)} %compare.26, f32[1024,1024,8]{1,0,2:T(8,128)} %get-tuple-element.354, f32[1024,8]{0,1:T(8,128)S(1)} %select_maximum_fusion.2, ...), kind=kOutput, calls=%fused_computation.10.clone.1 | convolution fusion | flops 2192572416 | bytes 43319300 | tf_op jit(solution)/shard_map/while/body/eval_jaxpr/thk,dk->thd/dot_general | solution.py:37
  204.2 1.2 compare_and_fusion.2
  205.4 14.9 %fusion.51 = (f32[1024,8]{0,1:T(8,128)S(1)}, f32[1024,1024,8]{1,0,2:T(8,128)}) fusion(pred[1024,1024]{0,1:T(8,128)(4,1)S(1)} %compare_and_fusion.2, bf16[1024,8,128]{2,0,1:T(8,128)(2,1)} %get-tuple-element.396, bf16[128,4096]{0,1:T(8,128)(2,1)} %get-tuple-element.395, s32[]{:T(128)S(6)} %select_n.226), kind=kOutput, calls=%fused_computation.4.clone.1 | convolution fusion | flops 2172641280 | bytes 36995076 | tf_op jit(solution)/shard_map/while/body/eval_jaxpr/thd,dk->thk/dot_general | solution.py:29
  220.3 14.7 %fusion.52 = f32[1024,8]{0,1:T(8,128)S(1)} fusion(f32[1024,1024,8]{1,0,2:T(8,128)} %get-tuple-element.354, f32[1024,8]{0,1:T(8,128)S(1)} %select_maximum_fusion.2, pred[1024,1024]{0,1:T(8,128)(4,1)S(1)} %compare_and_fusion.2), kind=kLoop, calls=%fused_computation.6.clone.1 | loop fusion | flops 41934848 | bytes 34668544 | tf_op jit(solution)/shard_map/while/body/eval_jaxpr/reduce_sum | solution.py:36
  235.0 18.3 %fusion.54 = f32[1024,8,128]{2,0,1:T(8,128)} fusion(f32[1024,8,128]{2,0,1:T(8,128)} %get-tuple-element.375, f32[1024,8]{0,1:T(8,128)S(1)} %get-tuple-element.356, pred[]{:T(512)S(6)} %compare.26, f32[1024,1024,8]{1,0,2:T(8,128)} %get-tuple-element.354, f32[1024,8]{0,1:T(8,128)S(1)} %select_maximum_fusion.2, ...), kind=kOutput, calls=%fused_computation.10.clone.1 | convolution fusion | flops 2192572416 | bytes 43319300 | tf_op jit(solution)/shard_map/while/body/eval_jaxpr/thk,dk->thd/dot_general | solution.py:37
  253.3 5.5 %copy.18 = f32[1024,8,128]{0,2,1:T(8,128)} copy(f32[1024,8,128]{2,0,1:T(8,128)} %get-tuple-element.190) | data formatting | bytes 8388608 | tf_op jit(solution)/shard_map/while | solution.py:65
  258.8 2.8 divide_convert_fusion
  261.6 26.2 %convolution_convert_fusion = bf16[1024,8192]{1,0:T(8,128)(2,1)} fusion(bf16[1024,1024]{0,1:T(8,128)(2,1)S(1)} %bitcast.43, bf16[1024,8192]{1,0:T(8,128)(2,1)} %param.11), kind=kOutput, calls=%fused_computation.26 | convolution fusion | flops 17188257792 | bytes 35651584 | tf_op jit(solution)/shard_map/dot_general | solution.py:118
  287.8 0.0 reduce-scatter.2.cloned.1.call-update
  287.8 0.0 copy-start.1
  287.9 169.2 %reduce-scatter.2.cloned.1.call-done = bf16[1024,1024]{1,0:T(8,128)(2,1)} async-done(((bf16[1024,8192]{1,0:T(8,128)(2,1)}), bf16[1024,1024]{1,0:T(8,128)(2,1)}) %reduce-scatter.2.cloned.1.call-update) | async-done | bytes 2097168 | tf_op jit(solution)/shard_map/reduce_scatter | solution.py:119
  457.0 0.0 copy-done.1
  (37 shorter events, 0.3 us)
Async XLA Ops:
  6.5 1.6 copy-start
  6.5 9.8 %copy-start.2 = (s32[4096]{0:T(1024)S(1)}, s32[4096]{0:T(1024)}, u32[]{:S(2)}) copy-start(s32[4096]{0:T(1024)} %param.13) | copy-start | bytes 49156
  6.5 51.0 %all-gather.2.cloned.1.call-start = ((), (), s32[]{:S(2)}) async-start(), calls=%async_computation.1 | async-start | bytes 1310720 | tf_op jit(solution)/shard_map/all_gather | solution.py:109
  9.0 448.0 %reduce-scatter.2.cloned.1.call-start = ((), (), s32[]{:S(2)}) async-start(), calls=%async_computation.2 | async-start | bytes 18874368 | tf_op jit(solution)/shard_map/reduce_scatter | solution.py:119
  10.8 11.7 %collective-permute-start = (bf16[128,1024]{1,0:T(8,128)(2,1)S(1)}, bf16[128,1024]{1,0:T(8,128)(2,1)S(1)}, u32[]{:S(2)}, u32[]{:S(2)}) collective-permute-start(bf16[128,1024]{1,0:T(8,128)(2,1)S(1)} %get-tuple-element.275), channel_id=1, source_target_pairs={{0,24},{8,0},{16,8},{24,16},{1,25},{9,1},{17,9},{25,17},{2,26},{10... | collective-permute-start | bytes 786440 | tf_op jit(solution)/shard_map/ppermute | solution.py:93
  23.4 29.6 %collective-permute-start.1 = (bf16[128,2048]{1,0:T(8,128)(2,1)}, bf16[128,2048]{1,0:T(8,128)(2,1)S(1)}, u32[]{:S(2)}, u32[]{:S(2)}) collective-permute-start(bf16[128,2048]{1,0:T(8,128)(2,1)} %pad_maximum_fusion), channel_id=1, source_target_pairs={{0,16},{8,24},{16,0},{24,8},{1,17},{9,25},{17,1},{25,9},{2,18},{10... | collective-permute-start | bytes 1572872 | tf_op jit(solution)/shard_map/ppermute | solution.py:93
  287.8 169.2 %copy-start.1 = (bf16[1024,1024]{1,0:T(8,128)(2,1)S(1)}, bf16[1024,1024]{1,0:T(8,128)(2,1)}, u32[]{:S(2)}) copy-start(bf16[1024,1024]{1,0:T(8,128)(2,1)} %param.9) | copy-start | bytes 6291460
Sparse Core Ops, SparseCore 0:
  9.2 33.6 all-gather.1
  288.0 169.0 reduce-scatter.1
